TPU v7x, 128 devices: a whole 4x4x4 slice. The times are simulated.
128 devices in a mesh: group: 2 (over y_hi), shard: 64 (over y_lo, z, x, core).
Axes of the slice: x: 4, y: 4 (y_hi: 2, y_lo: 2; y = y_hi * 2 + y_lo), z: 4, core: 2. Of those that a mesh axis runs over, the one named last changes fastest.
Arguments:
- image_tokens: bfloat16 [256, 256, 2432], P(('group', 'shard')), may hold values from -6 to 6
- image_gain: float32 [2432], replicated, may hold values from 0.1 to 1.9
- caption_states: bfloat16 [256, 384, 2432], P('group', None, 'shard'), may hold values from -6 to 6
- text_gain: float32 [2432], replicated, may hold values from 0.1 to 1.9
- lengths: int32 [2, 128], P('group'), may hold values from 1 to 333, as said below
- assign: int32 [2, 128], P('group'), may hold values from 0 to 127, as said below
- image_qkv: bfloat16 [2432, 3840], P(('group', 'shard')), may hold values from -0.125 to 0.125
- text_kv: bfloat16 [2432, 2560], P(('group', 'shard')), may hold values from -0.125 to 0.125
Outputs:
- attended: bfloat16 [256, 256, 1280], P(('group', 'shard'))
Inputs may be any that keep to these rules, and one draw needn't show every extreme that they name: Each row is a permutation: a half's trainer slots assign[g, s], 2 consecutive slots to each device of the half in order. `lengths`: caption rows at or beyond a sample's length are padding and take no part in attention. Counting ceil(length / 128) blocks of 128 rows for each sample, the 2 samples of one trainer device use exactly 4 blocks together.
All inputs are finite; a program needn't handle non-finite values.
Results may differ from a plain program's by a relative error of at most 0.0083.
Values may be sent and summed in bfloat16 or wider, within the bound.
A program may use at most 192 MiB of HBM per device.

v0:
```python
import functools

import jax
import jax.numpy as jnp
from jax import lax
from jax.experimental import pallas as pl
from jax.experimental.pallas import tpu as pltpu
from jax.sharding import Mesh, PartitionSpec as P

D = 2432
HW = 1280
FEAT = 38
PADF = 40
CHIPS = 64
DP = CHIPS * PADF
PAIRS = 5
ROWS = 512
HALF = 640
AXES = ("yh", "yl", "z", "x", "c")
CHIP_AXES = ("yh", "yl", "z", "x")
SHARD_AXES = ("yl", "z", "x", "c")
f32 = jnp.float32
bf16 = jnp.bfloat16


def compact_kernel(src_ref, blk_ref, x_ref, o_ref, sem):
    def copy(e):
        b = pl.multiple_of(blk_ref[e] * 128, 128)
        return pltpu.make_async_copy(
            x_ref.at[src_ref[e], :, pl.ds(b, 128)], o_ref.at[e], sem
        )

    @pl.loop(0, 256)
    def _(e):
        copy(e).start()

    pltpu.make_async_copy(o_ref, o_ref, sem).wait()


def compact(caps, src, blk):
    return pl.pallas_call(
        compact_kernel,
        out_shape=jax.ShapeDtypeStruct((256, PADF, 128), bf16),
        grid_spec=pltpu.PrefetchScalarGridSpec(
            num_scalar_prefetch=2,
            grid=(1,),
            in_specs=[pl.BlockSpec((128, PADF, 384), lambda i, a, b: (0, 0, 0))],
            out_specs=pl.BlockSpec(memory_space=pl.ANY),
            scratch_shapes=[pltpu.SemaphoreType.DMA],
        ),
        name="compact",
    )(src, blk, caps)


def layer_norm_rows(x, mask, gain):
    mean = jnp.sum(x, axis=1, keepdims=True) * (1.0 / D)
    d = x - mean
    if mask is not None:
        d = d * mask
    var = jnp.sum(d * d, axis=1, keepdims=True) * (1.0 / D)
    return (d * lax.rsqrt(var + 1e-06) * gain).astype(bf16)


def spread_block(o):
    first = 128 * o
    start = (first // PADF) * FEAT + min(first % PADF, FEAT)
    lo = min(start // 128 * 128, D - 256)
    r = lax.broadcasted_iota(jnp.int32, (256, 128), 0)
    col = lax.broadcasted_iota(jnp.int32, (256, 128), 1) + first
    blk = lax.div(col, PADF)
    off = col - blk * PADF
    hit = (r + lo == blk * FEAT + off) & (off < FEAT)
    return lo, jnp.where(hit, 1.0, 0.0).astype(bf16)


def image_kernel(x_ref, g_ref, o_ref):
    y = layer_norm_rows(x_ref[...].astype(f32), None, g_ref[...])
    for o in range(DP // 128):
        lo, s = spread_block(o)
        o_ref[:, 128 * o : 128 * o + 128] = jnp.dot(
            y[:, lo : lo + 256], s, preferred_element_type=f32
        ).astype(bf16)


def image_prep(x, gain):
    return pl.pallas_call(
        image_kernel,
        out_shape=jax.ShapeDtypeStruct((ROWS, DP), bf16),
        grid=(4,),
        in_specs=[
            pl.BlockSpec((128, D), lambda i: (i, 0)),
            pl.BlockSpec((1, D), lambda i: (0, 0)),
        ],
        out_specs=pl.BlockSpec((128, DP), lambda i: (i, 0)),
        cost_estimate=pl.CostEstimate(
            flops=2 * ROWS * 256 * DP, bytes_accessed=4 * ROWS * DP, transcendentals=0
        ),
        name="image_prep",
    )(x, gain.reshape(1, D))


def text_kernel(x_ref, g_ref, m_ref, o_ref):
    x = x_ref[:, 0].reshape(DP, 128)
    o_ref[...] = layer_norm_rows(
        jnp.transpose(x.astype(f32)), m_ref[...], g_ref[...]
    )


def text_prep(x, gain_row, mask_row):
    return pl.pallas_call(
        text_kernel,
        out_shape=jax.ShapeDtypeStruct((ROWS, DP), bf16),
        grid=(4,),
        in_specs=[
            pl.BlockSpec((CHIPS, 1, PADF, 128), lambda i: (0, i, 0, 0)),
            pl.BlockSpec((1, DP), lambda i: (0, 0)),
            pl.BlockSpec((1, DP), lambda i: (0, 0)),
        ],
        out_specs=pl.BlockSpec((128, DP), lambda i: (i, 0)),
        cost_estimate=pl.CostEstimate(
            flops=8 * ROWS * DP, bytes_accessed=4 * ROWS * DP, transcendentals=0
        ),
        name="text_prep",
    )(x, gain_row, mask_row)


def head_scale(y, ones):
    sq = y * y
    hi = sq.astype(bf16)
    lo = (sq - hi.astype(f32)).astype(bf16)
    total = jnp.dot(hi, ones, preferred_element_type=f32) + jnp.dot(
        lo, ones, preferred_element_type=f32
    )
    return y * lax.rsqrt(total * (1.0 / 64.0) + 1e-06)


def main_kernel(len_ref, x_ref, t_ref, w_ref, o_ref, q_s, k_s, v_s, tk_s, tv_s):
    def weights(i):
        return w_ref[:, i].reshape(DP, 128)

    a = lax.broadcasted_iota(jnp.int32, (256, 256), 0) // 64
    b = lax.broadcasted_iota(jnp.int32, (256, 256), 1) // 64
    ones = jnp.where(a == b, 1.0, 0.0).astype(bf16)

    qk = jnp.dot(
        x_ref[...],
        jnp.concatenate([weights(0), weights(1)], axis=1),
        preferred_element_type=f32,
    )
    qk = head_scale(qk, ones)
    q_s[...] = (qk[:, :128] * 0.125).astype(bf16)
    k_s[...] = qk[:, 128:].astype(bf16)
    v_s[...] = jnp.dot(x_ref[...], weights(2), preferred_element_type=f32).astype(bf16)
    tkv = jnp.dot(
        t_ref[...],
        jnp.concatenate([weights(3), weights(4)], axis=1),
        preferred_element_type=f32,
    )
    tk_s[...] = head_scale(tkv[:, :128], ones[:128, :128]).astype(bf16)
    tv_s[...] = tkv[:, 128:].astype(bf16)

    left = lax.broadcasted_iota(jnp.int32, (640, 128), 1) < 64
    zero = jnp.zeros((640, 128), bf16)
    one = jnp.ones((640, 128), bf16)
    row = lax.broadcasted_iota(jnp.int32, (384, 128), 0)

    for s in range(4):
        dev, j = s // 2, s % 2
        base = dev * ROWS + j * 128
        if j == 0:
            pos = row
        else:
            pos = (2 - row // 128) * 128 + row % 128
        live = pos < len_ref[s]
        q = q_s[pl.ds(s * 256, 256), :]
        k = jnp.concatenate(
            [k_s[pl.ds(s * 256, 256), :], tk_s[pl.ds(base, 384), :]], axis=0
        )
        v = jnp.concatenate(
            [
                v_s[pl.ds(s * 256, 256), :],
                jnp.where(live, tv_s[pl.ds(base, 384), :], 0).astype(bf16),
            ],
            axis=0,
        )
        n = jnp.concatenate(
            [one[:256], jnp.where(live, 1.0, 0.0).astype(bf16)], axis=0
        )
        kk = jnp.concatenate(
            [jnp.where(left, k, zero), jnp.where(left, zero, k)], axis=0
        )
        sc = lax.dot_general(
            q, kk, (((1,), (1,)), ((), ())), preferred_element_type=f32
        )
        p = jnp.exp(sc).astype(bf16)
        vv = jnp.concatenate(
            [
                jnp.concatenate([jnp.where(left, v, zero), jnp.where(left, n, zero)], 1),
                jnp.concatenate([jnp.where(left, zero, v), jnp.where(left, zero, n)], 1),
            ],
            axis=0,
        )
        o = jnp.dot(p, vv, preferred_element_type=f32)
        o_ref[pl.ds(s * 256, 256), :] = (o[:, :128] / o[:, 128:]).astype(bf16)


def main(lens, x, t, w):
    return pl.pallas_call(
        main_kernel,
        out_shape=jax.ShapeDtypeStruct((2 * ROWS, HALF), bf16),
        grid_spec=pltpu.PrefetchScalarGridSpec(
            num_scalar_prefetch=1,
            grid=(PAIRS,),
            in_specs=[
                pl.BlockSpec((2 * ROWS, DP), lambda i, a: (0, 0)),
                pl.BlockSpec((2 * ROWS, DP), lambda i, a: (0, 0)),
                pl.BlockSpec((CHIPS, 5, PADF, 128), lambda i, a: (0, i, 0, 0)),
            ],
            out_specs=pl.BlockSpec((2 * ROWS, 128), lambda i, a: (0, i)),
            scratch_shapes=[pltpu.VMEM((2 * ROWS, 128), bf16)] * 5,
        ),
        cost_estimate=pl.CostEstimate(
            flops=2 * 2 * ROWS * DP * 5 * 640,
            bytes_accessed=2 * DP * 3200 + 8 * ROWS * DP,
            transcendentals=4 * 2560 * 2560,
        ),
        compiler_params=pltpu.CompilerParams(vmem_limit_bytes=60 << 20),
        name="proj_attend",
    )(lens, x, t, w)


def chip_weights(image_qkv, text_kv, core):
    wi = image_qkv.reshape(19, 3, 2, PAIRS, 128)
    wt = text_kv.reshape(19, 2, 2, PAIRS, 128)
    w = jnp.concatenate([wi, wt], axis=1).transpose(2, 3, 1, 0, 4)
    w = w.reshape(2, 25, 19, 128)
    w = jnp.where(
        core == 0,
        jnp.pad(w, ((0, 0), (0, 0), (0, 21), (0, 0))),
        jnp.pad(w, ((0, 0), (0, 0), (19, 2), (0, 0))),
    )
    mine = jnp.where(core == 0, w[0], w[1])
    other = jnp.where(core == 0, w[1], w[0])
    return mine + lax.ppermute(other, "c", [(0, 1), (1, 0)])


def shards(
    image_tokens, image_gain, caption_states, text_gain, lengths, assign, image_qkv, text_kv
):
    core = lax.axis_index("c")
    chip = lax.axis_index(("yl", "z", "x"))

    w = lax.all_gather(chip_weights(image_qkv, text_kv, core), CHIP_AXES, axis=0)

    places = jnp.arange(128, dtype=jnp.int32)
    match = assign[0][:, None] == places[None, :]
    inverse = jnp.sum(jnp.where(match, places[:, None], 0), axis=0)
    ordered = jnp.sum(jnp.where(match, lengths[0][:, None], 0), axis=0)
    pair_src = inverse.reshape(64, 2)
    first = (ordered.reshape(64, 2)[:, :1] + 127) // 128
    slot = jnp.arange(4, dtype=jnp.int32)[None, :]
    own = slot < first
    src = jnp.where(own, pair_src[:, :1], pair_src[:, 1:]).reshape(256)
    blk = jnp.clip(jnp.where(own, slot, 3 - slot), 0, 2).reshape(256)
    lens = lax.dynamic_slice_in_dim(ordered, chip * 4, 4, 0)

    caps = jnp.pad(jnp.transpose(caption_states, (0, 2, 1)), ((0, 0), (0, 2), (0, 0)))
    caps = compact(caps, src, blk).reshape(64, 4, PADF, 128)
    caps = lax.all_to_all(caps, SHARD_AXES, split_axis=0, concat_axis=0, tiled=True)

    def spread_row(v):
        return jnp.pad(v.reshape(CHIPS, FEAT), ((0, 0), (0, 2))).reshape(1, DP)

    mask_row = spread_row(jnp.ones((D,), f32))
    t = text_prep(caps, spread_row(text_gain), mask_row)
    x = image_prep(image_tokens.reshape(ROWS, D), image_gain)
    x = lax.all_gather(x, "c", axis=0, tiled=True)
    t = lax.all_gather(t, "c", axis=0, tiled=True)
    out = main(lens, x, t, w)
    out = lax.all_to_all(
        out.reshape(2, ROWS, HALF), "c", split_axis=0, concat_axis=0, tiled=True
    )
    return jnp.concatenate([out[0], out[1]], axis=1).reshape(2, 256, HW)


def solution(mesh):
    fine = Mesh(mesh.devices.reshape(2, 2, 4, 4, 2), AXES)
    full = P(AXES)
    placed = (
        P(AXES, None, None),
        P(),
        P("yh", None, SHARD_AXES),
        P(),
        P("yh", None),
        P("yh", None),
        P(AXES, None),
        P(AXES, None),
    )
    return jax.shard_map(
        shards,
        mesh=fine,
        in_specs=placed,
        out_specs=P(AXES, None, None),
        check_vma=False,
    )
```

profile of v0, /device:TPU:1, one launch (start us, length us, event | category | flops | bytes accessed | tf_op | source)
XLA Modules:
  0.0 268.9 jit_solution(6415959311721541151)
XLA Ops:
  6.5 1.3 reshape.66.g_ref
  7.8 6.1 %image_prep.1 = bf16[512,2560]{1,0:T(8,128)(2,1)} custom-call(bf16[512,2432]{1,0:T(8,128)(2,1)} %bitcast.23, f32[1,2432]{1,0:T(1,128)} %reshape.66.g_ref), custom_call_target="tpu_custom_call" | custom-call | flops 671088640 | bytes 5242880 | tf_op jit(solution)/shard_map/image_prep/pallas_call | solution.py:86
  13.9 0.0 all-gather.5.cloned.1.call-update
  14.0 0.1 lt.30
  14.1 0.1 broadcast_in_dim.74
  14.2 0.4 copy-done.4
  14.6 0.1 select_reduce_fusion
  14.7 0.1 reshape.67
  14.9 0.1 fusion.1
  15.0 0.1 lt.32
  15.1 0.1 lt.33
  15.2 0.1 reshape.68
  15.3 0.2 slice_reduce_fusion
  15.5 0.1 broadcast_in_dim.68
  15.6 0.1 broadcast_in_dim.69
  15.7 0.1 broadcast_in_dim.71
  15.8 0.1 broadcast_in_dim.72
  15.9 4.3 %copy.31 = bf16[128,384,38]{1,2,0:T(8,128)(2,1)S(1)} copy(bf16[128,384,38]{1,0,2:T(8,128)(2,1)} %param.10) | data formatting | bytes 7471104 | tf_op args[2]
  20.2 2.3 pad.21.x_ref
  22.4 0.6 select_clamp_fusion
  23.0 5.3 %compact.1 = bf16[256,40,128]{2,1,0:T(8,128)(2,1)} custom-call(s32[256]{0:T(256)} %get-tuple-element.14.src_ref, s32[256]{0:T(256)} %get-tuple-element.13.blk_ref, bf16[128,40,384]{2,1,0:T(8,128)(2,1)} %pad.21.x_ref), custom_call_target="tpu_custom_call" | custom-call | tf_op jit(solution)/shard_map/compact/pallas_call | solution.py:41
  28.4 11.4 %all-to-all-start = ((bf16[64,4,40,128]{3,2,1,0:T(8,128)(2,1)}), bf16[64,4,40,128]{3,2,1,0:T(8,128)(2,1)S(1)}, u32[]{:S(2)}, u32[]{:S(2)}) async-start(bf16[64,4,40,128]{3,2,1,0:T(8,128)(2,1)} %bitcast.20), calls=%async_computation | async-start | bytes 5242880 | tf_op jit(solution)/shard_map/all_to_all | solution.py:269
  39.8 0.0 all-gather.7.cloned.1.call-start
  39.8 0.1 reshape.70
  40.0 0.7 reshape.71.g_ref
  40.7 0.7 reshape.73.m_ref
  41.4 32.1 %all-to-all-done.x_ref = bf16[64,4,40,128]{3,2,1,0:T(8,128)(2,1)S(1)} async-done(((bf16[64,4,40,128]{3,2,1,0:T(8,128)(2,1)}), bf16[64,4,40,128]{3,2,1,0:T(8,128)(2,1)S(1)}, u32[]{:S(2)}, u32[]{:S(2)}) %all-to-all-start) | async-done | bytes 2621472 | tf_op jit(solution)/shard_map/all_to_all | solution.py:269
  73.5 1.5 copy-done
  75.0 5.4 %text_prep.1 = bf16[512,2560]{1,0:T(8,128)(2,1)} custom-call(bf16[64,4,40,128]{3,2,1,0:T(8,128)(2,1)} %copy-done, f32[1,2560]{1,0:T(1,128)} %reshape.71.g_ref, f32[1,2560]{1,0:T(1,128)} %reshape.73.m_ref), custom_call_target="tpu_custom_call" | custom-call | flops 10485760 | bytes 5242880 | tf_op jit(solution)/shard_map/text_prep/pallas_call | solution.py:110
  80.5 0.0 all-gather.9.cloned.1.call-start
  80.5 0.8 copy-done.2
  81.3 0.1 reshape.75
  81.5 0.2 reshape.74
  81.7 0.1 maximum_bitcast_fusion
  81.8 0.2 copy.25
  82.0 0.5 broadcast_select_fusion
  82.5 1.2 broadcast_select_fusion.2
  83.7 1.1 collective-permute-start
  84.8 1.2 collective-permute-done
  85.9 0.7 bitcast_add_fusion
  86.7 0.0 all-gather.9.cloned.1.call-update
  86.7 0.6 dynamic_slice.3.len_ref
  87.3 11.1 %all-gather.7.cloned.1.call-done.t_ref = bf16[1024,2560]{1,0:T(8,128)(2,1)} async-done(((bf16[512,2560]{1,0:T(8,128)(2,1)}), bf16[1024,2560]{1,0:T(8,128)(2,1)}) %all-gather.7.cloned.1.call-update) | async-done | bytes 5242896 | tf_op jit(solution)/shard_map/all_gather | solution.py:278
  98.4 106.3 %all-gather.9.cloned.1.call-done = bf16[1600,40,128]{2,1,0:T(8,128)(2,1)} async-done(((bf16[25,40,128]{2,1,0:T(8,128)(2,1)}), bf16[1600,40,128]{2,1,0:T(8,128)(2,1)}) %all-gather.9.cloned.1.call-update) | async-done | bytes 16384016 | tf_op jit(solution)/shard_map/all_gather | solution.py:253
  204.7 50.0 %proj_attend.1 = bf16[1024,640]{1,0:T(8,128)(2,1)} custom-call(s32[4]{0:T(128)} %dynamic_slice.3.len_ref, bf16[1024,2560]{1,0:T(8,128)(2,1)} %all-gather.5.cloned.1.call-done.x_ref, bf16[1024,2560]{1,0:T(8,128)(2,1)} %all-gather.7.cloned.1.call-done.t_ref, bf16[64,25,40,128]{3,2,1,0:T(8,128)(2,1)} %bitcast.29), custom_call_target="tpu_custom_call" | custom-call | flops 16777216000 | bytes 26869760 | tf_op jit(solution)/shard_map/proj_attend/pallas_call | solution.py:208
  254.7 6.4 %all_to_all.10 = bf16[2,512,640]{2,1,0:T(8,128)(2,1)S(1)} all-to-all(bf16[2,512,640]{2,1,0:T(8,128)(2,1)} %bitcast.24), channel_id=1, replica_groups=mesh['yh'=2,'yl'=2,'z'=4,'x'=4,'c'=2] {'c'}, dimensions={0} | all-to-all | bytes 2621440 | tf_op jit(solution)/shard_map/all_to_all | solution.py:280
  261.1 0.1 fusion.3
  261.2 1.2 pad_maximum_fusion
  (20 shorter events, 0.1 us)
Async XLA Ops:
  6.5 80.8 %all-gather.5.cloned.1.call-start = ((), (), s32[]{:S(2)}) async-start(), calls=%async_computation.2 | async-start | bytes 7864320 | tf_op jit(solution)/shard_map/all_gather | solution.py:277
  13.9 0.7 copy-start.4
  13.9 0.7 copy-start.5
  28.3 11.5 %copy-start.3 = (f32[2432]{0:T(1024)S(1)}, f32[2432]{0:T(1024)}, u32[]{:S(2)}) copy-start(f32[2432]{0:T(1024)} %param.11) | copy-start | bytes 29188
  28.4 45.1 %all-to-all-start = ((bf16[64,4,40,128]{3,2,1,0:T(8,128)(2,1)}), bf16[64,4,40,128]{3,2,1,0:T(8,128)(2,1)S(1)}, u32[]{:S(2)}, u32[]{:S(2)}) async-start(bf16[64,4,40,128]{3,2,1,0:T(8,128)(2,1)} %bitcast.20), calls=%async_computation | async-start | bytes 5242880 | tf_op jit(solution)/shard_map/all_to_all | solution.py:269
  39.8 58.7 %all-gather.7.cloned.1.call-start = ((), (), s32[]{:S(2)}) async-start(), calls=%async_computation.3 | async-start | bytes 7864320 | tf_op jit(solution)/shard_map/all_gather | solution.py:278
  73.5 1.5 copy-start
  80.4 0.9 copy-start.2
  80.4 1.0 copy-start.1
  80.5 124.2 %all-gather.9.cloned.1.call-start = ((), (), s32[]{:S(2)}) async-start(), calls=%async_computation.4 | async-start | bytes 16640000 | tf_op jit(solution)/shard_map/all_gather | solution.py:253
  83.7 2.2 collective-permute-start
Sparse Core Ops, SparseCore 0:
  14.1 21.5 all-gather.4
  80.6 17.8 all-gather.6
  101.2 103.4 all-gather.8
where the time goes:
time: 270 us; the launch traced here: 269 us
  waiting for transfers between devices  151 us (56%)
  Pallas kernels  66.8 us (25%)
  local copies, waits for them, and re-layouts  14.7 us (5%)
  between operations  13.3 us (5%)
  starting transfers between devices  12.5 us (5%)
  blocking collectives  6.38 us (2%)
  other arithmetic  4.51 us (2%)
    all_gather x1, waiting for transfers between devices, shards(): lax.all_gather(chip_weights(image_qkv, text_kv, core), CHIP_AXES, axis=0)  106 us
    pallas_call x1, Pallas kernels, main(): pl.pallas_call(main_kernel, out_shape=jax.ShapeDtypeStruct((2 * ROWS, HAL...  50 us
    all_to_all x1, waiting for transfers between devices, shards(): lax.all_to_all(caps, SHARD_AXES, split_axis=0, concat_axis=0, tiled=True)  32.1 us
    all_to_all x1, starting transfers between devices, shards(): lax.all_to_all(caps, SHARD_AXES, split_axis=0, concat_axis=0, tiled=True)  11.4 us
    all_gather x1, waiting for transfers between devices, shards(): t = lax.all_gather(t, 'c', axis=0, tiled=True)  11.1 us
    unnamed x14, local copies, waits for them, and re-layouts  7.07 us
    all_to_all x1, blocking collectives, shards(): lax.all_to_all(out.reshape(2, ROWS, HALF), 'c', split_axis=0, concat_axis...  6.38 us
    pallas_call x1, Pallas kernels, image_prep(): pl.pallas_call(image_kernel, out_shape=jax.ShapeDtypeStruct((ROWS, DP), b...  6.08 us
  transfers between devices with their start and end apart: 5, of which 4 were waited for; matrix products, arithmetic and copies ran while one was open for 5% of the time, Pallas kernels for 4%

commit v1 on v0

v1 whole, which is shorter than its diff:
```python
import functools

import jax
import jax.numpy as jnp
from jax import lax
from jax.experimental import pallas as pl
from jax.experimental.pallas import tpu as pltpu
from jax.sharding import Mesh, PartitionSpec as P

D = 2432
HW = 1280
FEAT = 38
PADF = 40
CHIPS = 64
DP = CHIPS * PADF
PAIRS = 5
ROWS = 512
HALF = 640
AXES = ("yh", "yl", "z", "x", "c")
CHIP_AXES = ("yh", "yl", "z", "x")
SHARD_AXES = ("yl", "z", "x", "c")
f32 = jnp.float32
bf16 = jnp.bfloat16


DIMS = (("x", "z", "y"), ("z", "y", "x"), ("y", "x", "z"))
STEPS = 9
MESH = pl.DeviceIdType.MESH


def layer_norm_rows(x, mask, gain):
    mean = jnp.sum(x, axis=1, keepdims=True) * (1.0 / D)
    d = x - mean
    if mask is not None:
        d = d * mask
    var = jnp.sum(d * d, axis=1, keepdims=True) * (1.0 / D)
    return (d * lax.rsqrt(var + 1e-06) * gain).astype(bf16)


def spread_low(o):
    first = 128 * o
    start = (first // PADF) * FEAT + min(first % PADF, FEAT)
    return min(start // 128 * 128, D - 256)


def spread_block(o):
    first = 128 * o
    lo = spread_low(o)
    r = lax.broadcasted_iota(jnp.int32, (256, 128), 0)
    col = lax.broadcasted_iota(jnp.int32, (256, 128), 1) + first
    blk = lax.div(col, PADF)
    off = col - blk * PADF
    hit = (r + lo == blk * FEAT + off) & (off < FEAT)
    return lo, jnp.where(hit, 1.0, 0.0).astype(bf16)


def head_scale(y, ones):
    sq = y * y
    hi = sq.astype(bf16)
    lo = (sq - hi.astype(f32)).astype(bf16)
    total = jnp.dot(hi, ones, preferred_element_type=f32) + jnp.dot(
        lo, ones, preferred_element_type=f32
    )
    return y * lax.rsqrt(total * (1.0 / 64.0) + 1e-06)


def attend(len_ref, s, q_s, k_s, v_s, tk_s, tv_s):
    left = lax.broadcasted_iota(jnp.int32, (640, 128), 1) < 64
    zero = jnp.zeros((640, 128), bf16)
    row = lax.broadcasted_iota(jnp.int32, (384, 128), 0)
    dev, j = s // 2, s % 2
    base = dev * ROWS + j * 128
    pos = row if j == 0 else (2 - row // 128) * 128 + row % 128
    live = pos < len_ref[s]
    q = q_s[pl.ds(s * 256, 256), :]
    k = jnp.concatenate(
        [k_s[pl.ds(s * 256, 256), :], tk_s[pl.ds(base, 384), :]], axis=0
    )
    v = jnp.concatenate(
        [
            v_s[pl.ds(s * 256, 256), :],
            jnp.where(live, tv_s[pl.ds(base, 384), :], 0).astype(bf16),
        ],
        axis=0,
    )
    n = jnp.concatenate(
        [jnp.ones((256, 128), bf16), jnp.where(live, 1.0, 0.0).astype(bf16)], axis=0
    )
    kk = jnp.concatenate([jnp.where(left, k, zero), jnp.where(left, zero, k)], axis=0)
    sc = lax.dot_general(q, kk, (((1,), (1,)), ((), ())), preferred_element_type=f32)
    p = jnp.exp(sc).astype(bf16)
    vv = jnp.concatenate(
        [
            jnp.concatenate([jnp.where(left, v, zero), jnp.where(left, n, zero)], 1),
            jnp.concatenate([jnp.where(left, zero, v), jnp.where(left, zero, n)], 1),
        ],
        axis=0,
    )
    o = jnp.dot(p, vv, preferred_element_type=f32)
    return (o[:, :128] / o[:, 128:]).astype(bf16)


def fused_kernel(
    src_ref, blk_ref, len_ref, u_hbm, caps_hbm, img_hbm, ig_ref, tg_ref, tm_ref,
    out_hbm,
    w, caps, cc, land, img, xs, ts, spread, o_s, q_s, k_s, v_s, tk_s, tv_s,
    in_sem, s12, r12, s3, r3, a2a_s, a2a_r, px_s, px_r, po_s, po_r, po_l,
):
    yh, yl, z, x, c = (lax.axis_index(a) for a in AXES)
    y = yh * 2 + yl
    at = {"y": y, "z": z, "x": x}

    def device(y_, z_, x_, c_):
        return (y_ // 2, y_ % 2, z_, x_, c_)

    def ring(dim, delta):
        pos = dict(at)
        pos[dim] = (pos[dim] + delta) % 4
        return device(pos["y"], pos["z"], pos["x"], c)

    partner = device(y, z, x, 1 - c)

    def view(phase, color, idx, part=None, a=None):
        count = 9 if color == 0 else 8
        if phase == 2:
            sub = slice(None) if part is None else pl.ds(2 * part, 2)
            if color == 0:
                return w.at[a, 0, idx, sub]
            if color == 1:
                return w.at[a, 1, sub, :, idx]
            return w.at[a, 2, sub, idx]
        if part is None:
            rows = pl.ds(0, count)
        elif part == 0:
            rows = pl.ds(0, (count + 1) // 2)
        else:
            rows = pl.ds((count + 1) // 2, count // 2)
        if phase == 0:
            if color == 0:
                return w.at[rows, 0, y, z, idx]
            if color == 1:
                return w.at[rows, 1, y, idx, x]
            return w.at[rows, 2, idx, z, x]
        if color == 0:
            return w.at[rows, 0, y, idx]
        if color == 1:
            return w.at[rows, 1, idx, :, x]
        return w.at[rows, 2, :, z, idx]

    def message(phase, color, kind, a, shift, part):
        dim = DIMS[color][phase]
        block = view(phase, color, (at[dim] + shift) % 4, part, a)
        if phase == 2:
            send, recv = s3.at[a, color, kind], r3.at[a, color, kind]
        else:
            send, recv = s12.at[phase, color, kind], r12.at[phase, color, kind]
        return pltpu.make_async_remote_copy(
            src_ref=block,
            dst_ref=block,
            send_sem=send,
            recv_sem=recv,
            device_id=ring(dim, 1 if kind % 2 == 0 else -1),
            device_id_type=MESH,
        )

    out_shift = (0, 0, 3, 1)
    in_shift = (3, 1, 2, 2)
    parts = (None, None, 0, 1)

    def each_color(phase, a, f):
        if phase == 2:
            f(0)

            @pl.when(a < 8)
            def _():
                f(1)
                f(2)
        else:
            for color in range(3):
                f(color)

    def send(phase, step, a=None):
        def f(color):
            for kind in (2 * step, 2 * step + 1):
                message(phase, color, kind, a, out_shift[kind], parts[kind]).start()

        each_color(phase, a, f)

    def arrive(phase, step, a=None):
        def f(color):
            for kind in (2 * step, 2 * step + 1):
                message(phase, color, kind, a, in_shift[kind], parts[kind]).wait_recv()

        each_color(phase, a, f)

    def sent(phase, a=None):
        def f(color):
            for kind in range(4):
                message(phase, color, kind, a, out_shift[kind], parts[kind]).wait_send()

        each_color(phase, a, f)

    def advance(a):
        @pl.when(a < STEPS)
        def _():
            arrive(2, 0, a)
            send(2, 1, a)

        @pl.when(a + 2 < STEPS)
        def _():
            send(2, 0, a + 2)

    load_u = pltpu.make_async_copy(u_hbm, w.at[:, :, y, z, x], in_sem.at[0])
    load_caps = pltpu.make_async_copy(caps_hbm, caps, in_sem.at[1])
    load_img = pltpu.make_async_copy(img_hbm, img, in_sem.at[2])
    load_u.start()
    load_caps.start()
    load_img.start()

    me = (yl * 16 + z * 4 + x) * 2 + c

    def peer(k):
        j = (me + k) % 64
        return j, (yh, j // 32, (j // 8) % 4, (j // 2) % 4, j % 2)

    barrier = pltpu.get_barrier_semaphore()

    @pl.loop(1, 64)
    def _(k):
        pl.semaphore_signal(barrier, inc=1, device_id=peer(k)[1], device_id_type=MESH)

    across = (1 - yh, 1 - yl, z, x, c)
    pl.semaphore_signal(barrier, inc=1, device_id=across, device_id_type=MESH)

    for o in range(DP // 128):
        spread[o] = spread_block(o)[1]
    load_u.wait()
    pl.semaphore_wait(barrier, 64)

    send(0, 0)

    load_caps.wait()

    @pl.loop(0, 64)
    def _(d):
        for i in range(4):
            e = d * 4 + i
            b = blk_ref[e]
            rows = caps[src_ref[e]]
            cc[d, i, pl.ds(0, FEAT), :] = jnp.where(
                b == 0,
                rows[:, :128],
                jnp.where(b == 1, rows[:, 128:256], rows[:, 256:]),
            )
            cc[d, i, pl.ds(FEAT, 2), :] = jnp.zeros((2, 128), bf16)

    def exchange(k):
        j, dev = peer(k)
        return pltpu.make_async_remote_copy(
            src_ref=cc.at[j],
            dst_ref=land.at[me],
            send_sem=a2a_s,
            recv_sem=a2a_r,
            device_id=dev,
            device_id_type=MESH,
        )

    keep = pltpu.make_async_copy(cc.at[me], land.at[me], in_sem.at[3])
    keep.start()

    @pl.loop(1, 64)
    def _(k):
        exchange(k).start()

    arrive(0, 0)
    send(0, 1)
    load_img.wait()

    def image_chunk(i):
        rows = pl.ds(i * 128, 128)
        y_n = layer_norm_rows(img[rows, :].astype(f32), None, ig_ref[...])
        for o in range(DP // 128):
            lo = spread_low(o)
            xs[c, rows, 128 * o : 128 * o + 128] = jnp.dot(
                y_n[:, lo : lo + 256], spread[o], preferred_element_type=f32
            ).astype(bf16)

    @pl.loop(0, 2)
    def _(i):
        image_chunk(i)

    arrive(0, 1)
    send(1, 0)

    @pl.loop(2, 4)
    def _(i):
        image_chunk(i)

    def hand_over(buf, n):
        return pltpu.make_async_remote_copy(
            src_ref=buf.at[c],
            dst_ref=buf.at[c],
            send_sem=px_s.at[n],
            recv_sem=px_r.at[n],
            device_id=partner,
            device_id_type=MESH,
        )

    def take_over(buf, n):
        return pltpu.make_async_remote_copy(
            src_ref=buf.at[1 - c],
            dst_ref=buf.at[1 - c],
            send_sem=px_s.at[n],
            recv_sem=px_r.at[n],
            device_id=partner,
            device_id_type=MESH,
        )

    hand_over(xs, 0).start()
    arrive(1, 0)
    send(1, 1)
    arrive(1, 1)
    send(2, 0, 0)
    send(2, 0, 1)

    keep.wait()
    others = land.at[pl.ds(0, 63)]
    pltpu.make_async_copy(others, others, a2a_r).wait()

    @pl.loop(0, 4)
    def _(i):
        raw = land[:, i].reshape(DP, 128)
        ts[c, pl.ds(i * 128, 128), :] = layer_norm_rows(
            jnp.transpose(raw.astype(f32)), tm_ref[...], tg_ref[...]
        )

    hand_over(ts, 1).start()
    advance(0)
    advance(1)
    take_over(xs, 0).wait_recv()
    take_over(ts, 1).wait_recv()

    a_ = lax.broadcasted_iota(jnp.int32, (256, 256), 0) // 64
    b_ = lax.broadcasted_iota(jnp.int32, (256, 256), 1) // 64
    ones = jnp.where(a_ == b_, 1.0, 0.0).astype(bf16)

    def own_part(p):
        cols = pl.ds(pl.multiple_of(c * HALF + p * 128, 128), 128)
        return pltpu.make_async_copy(o_s.at[p, c], out_hbm.at[:, cols], po_l.at[p])

    def their_part(p, core):
        cols = pl.ds(pl.multiple_of(core * HALF + p * 128, 128), 128)
        return pltpu.make_async_remote_copy(
            src_ref=o_s.at[p, 1 - c],
            dst_ref=out_hbm.at[:, cols],
            send_sem=po_s.at[p],
            recv_sem=po_r.at[p],
            device_id=partner,
            device_id_type=MESH,
        )

    @pl.loop(0, PAIRS)
    def _(p):
        def weights(i):
            n = p * 5 + i
            return w[n // 3, n % 3].reshape(DP, 128)

        arrive(2, 1, 2 * p)

        @pl.when(2 * p + 1 < STEPS)
        def _():
            arrive(2, 1, 2 * p + 1)

        act = xs[...].reshape(2 * ROWS, DP)
        qk = jnp.dot(
            act,
            jnp.concatenate([weights(0), weights(1)], axis=1),
            preferred_element_type=f32,
        )
        qk = head_scale(qk, ones)
        q_s[...] = (qk[:, :128] * 0.125).astype(bf16)
        k_s[...] = qk[:, 128:].astype(bf16)
        advance(2 * p + 2)
        v_s[...] = jnp.dot(act, weights(2), preferred_element_type=f32).astype(bf16)
        tkv = jnp.dot(
            ts[...].reshape(2 * ROWS, DP),
            jnp.concatenate([weights(3), weights(4)], axis=1),
            preferred_element_type=f32,
        )
        tk_s[...] = head_scale(tkv[:, :128], ones[:128, :128]).astype(bf16)
        tv_s[...] = tkv[:, 128:].astype(bf16)
        advance(2 * p + 3)
        for s in range(4):
            o_s[p, s // 2, pl.ds(s % 2 * 256, 256), :] = attend(
                len_ref, s, q_s, k_s, v_s, tk_s, tv_s
            )
        own_part(p).start()
        their_part(p, c).start()

    @pl.loop(0, PAIRS)
    def _(p):
        own_part(p).wait()
        their_part(p, c).wait_send()
        their_part(p, 1 - c).wait_recv()

    hand_over(xs, 0).wait_send()
    hand_over(ts, 1).wait_send()
    sent(0)
    sent(1)

    @pl.loop(0, STEPS)
    def _(a):
        sent(2, a)

    pltpu.make_async_copy(others, others, a2a_s).wait()


def fused(src, blk, lens, u, caps, img, ig, tg, tm):
    hbm = pl.BlockSpec(memory_space=pl.ANY)
    vmem = pl.BlockSpec(memory_space=pltpu.VMEM)
    smem = pl.BlockSpec(memory_space=pltpu.SMEM)
    dma = pltpu.SemaphoreType.DMA
    head = pltpu.VMEM((2 * ROWS, 128), bf16)
    return pl.pallas_call(
        fused_kernel,
        out_shape=jax.ShapeDtypeStruct((ROWS, HW), bf16),
        in_specs=[smem, smem, smem, hbm, hbm, hbm, vmem, vmem, vmem],
        out_specs=hbm,
        scratch_shapes=[
            pltpu.VMEM((9, 3, 4, 4, 4, PADF, 128), bf16),
            pltpu.VMEM((128, FEAT, 384), bf16),
            pltpu.VMEM((64, 4, PADF, 128), bf16),
            pltpu.VMEM((64, 4, PADF, 128), bf16),
            pltpu.VMEM((ROWS, D), bf16),
            pltpu.VMEM((2, ROWS, DP), bf16),
            pltpu.VMEM((2, ROWS, DP), bf16),
            pltpu.VMEM((DP // 128, 256, 128), bf16),
            pltpu.VMEM((PAIRS, 2, ROWS, 128), bf16),
            head, head, head, head, head,
            dma((4,)),
            dma((2, 3, 4)), dma((2, 3, 4)),
            dma((9, 3, 4)), dma((9, 3, 4)),
            dma, dma,
            dma((2,)), dma((2,)),
            dma((PAIRS,)), dma((PAIRS,)), dma((PAIRS,)),
        ],
        compiler_params=pltpu.CompilerParams(
            collective_id=0, has_side_effects=True, vmem_limit_bytes=63 << 20
        ),
        name="joint_attention",
    )(src, blk, lens, u, caps, img, ig, tg, tm)


def chip_weights(image_qkv, text_kv, core):
    wi = image_qkv.reshape(19, 3, 2, PAIRS, 128)
    wt = text_kv.reshape(19, 2, 2, PAIRS, 128)
    w = jnp.concatenate([wi, wt], axis=1).transpose(2, 3, 1, 0, 4)
    w = w.reshape(2, 25, 19, 128)
    w = jnp.where(
        core == 0,
        jnp.pad(w, ((0, 0), (0, 0), (0, 21), (0, 0))),
        jnp.pad(w, ((0, 0), (0, 0), (19, 2), (0, 0))),
    )
    mine = jnp.where(core == 0, w[0], w[1])
    other = jnp.where(core == 0, w[1], w[0])
    return mine + lax.ppermute(other, "c", [(0, 1), (1, 0)])


def shards(
    image_tokens, image_gain, caption_states, text_gain, lengths, assign, image_qkv, text_kv
):
    core = lax.axis_index("c")
    chip = lax.axis_index(("yl", "z", "x"))
    u = chip_weights(image_qkv, text_kv, core)
    u = jnp.pad(u, ((0, 2), (0, 0), (0, 0))).reshape(9, 3, PADF, 128)

    places = jnp.arange(128, dtype=jnp.int32)
    match = assign[0][:, None] == places[None, :]
    inverse = jnp.sum(jnp.where(match, places[:, None], 0), axis=0)
    ordered = jnp.sum(jnp.where(match, lengths[0][:, None], 0), axis=0)
    pair_src = inverse.reshape(64, 2)
    first = (ordered.reshape(64, 2)[:, :1] + 127) // 128
    slot = jnp.arange(4, dtype=jnp.int32)[None, :]
    own = slot < first
    src = jnp.where(own, pair_src[:, :1], pair_src[:, 1:]).reshape(256)
    blk = jnp.clip(jnp.where(own, slot, 3 - slot), 0, 2).reshape(256)
    lens = lax.dynamic_slice_in_dim(ordered, chip * 4, 4, 0)

    def spread_row(v):
        return jnp.pad(v.reshape(CHIPS, FEAT), ((0, 0), (0, 2))).reshape(1, DP)

    out = fused(
        src, blk, lens, u,
        jnp.transpose(caption_states, (0, 2, 1)),
        image_tokens.reshape(ROWS, D),
        image_gain.reshape(1, D),
        spread_row(text_gain),
        spread_row(jnp.ones((D,), f32)),
    )
    return out.reshape(2, 256, HW)


def solution(mesh):
    fine = Mesh(mesh.devices.reshape(2, 2, 4, 4, 2), AXES)
    full = P(AXES)
    placed = (
        P(AXES, None, None),
        P(),
        P("yh", None, SHARD_AXES),
        P(),
        P("yh", None),
        P("yh", None),
        P(AXES, None),
        P(AXES, None),
    )
    return jax.shard_map(
        shards,
        mesh=fine,
        in_specs=placed,
        out_specs=P(AXES, None, None),
        check_vma=False,
    )
```

time: 270 us -> 162 us (0.60)
  waiting for transfers between devices: 151 us -> 0.01 us
  Pallas kernels: 66.8 us -> 142 us
  between operations: 13.3 us -> 0.2 us
  starting transfers between devices: 12.5 us -> 1.46 us
  blocking collectives: 6.38 us -> 0 us
    all_gather x3 -> x0, waiting for transfers between devices: 117 us -> none  [the longest x1 106 us: shards(): lax.all_gather(chip_weights(image_qkv, text_kv, core), CHIP_AXES, axis=0)]
    pallas_call x4 -> x1, Pallas kernels: 66.8 us -> 142 us  [fused(): pl.pallas_call(fused_kernel, out_shape=jax.ShapeDtypeStruct((ROWS, HW), b...]
    all_to_all x1 -> x0, waiting for transfers between devices: 32.1 us -> none  [shards(): lax.all_to_all(caps, SHARD_AXES, split_axis=0, concat_axis=0, tiled=True)]
    all_to_all x1 -> x0, starting transfers between devices: 11.4 us -> none  [shards(): lax.all_to_all(caps, SHARD_AXES, split_axis=0, concat_axis=0, tiled=True)]
    all_to_all x1 -> x0, blocking collectives: 6.38 us -> none  [shards(): lax.all_to_all(out.reshape(2, ROWS, HALF), 'c', split_axis=0, concat_axis...]
    unnamed x14 -> x11, local copies, waits for them, and re-layouts: 7.07 us -> 8.67 us
  transfers between devices with their start and end apart: 5 -> 1, of which waited for: 4 -> 0; matrix products, arithmetic and copies ran while one was open for 5% -> 7% of each run, Pallas kernels for 4% -> 0%
where the time goes in v1:
time: 162 us
  Pallas kernels  142 us (88%)
  local copies, waits for them, and re-layouts  15.7 us (10%)
  other arithmetic  2.68 us (2%)
    pallas_call x1, Pallas kernels, fused(): pl.pallas_call(fused_kernel, out_shape=jax.ShapeDtypeStruct((ROWS, HW), b...  142 us
    unnamed x11, local copies, waits for them, and re-layouts  8.67 us
  transfers between devices with their start and end apart: 1, of which 0 were waited for; matrix products, arithmetic and copies ran while one was open for 7% of the time, Pallas kernels for 0%

profile of v1, /device:TPU:1, one launch (start us, length us, event | category | flops | bytes accessed | tf_op | source)
XLA Modules:
  0.0 161.8 jit_solution(9934957023293109211)
XLA Ops:
  0.0 1.0 reshape.63
  1.0 1.1 reshape.62
  2.2 0.0 copy-start.2
  2.2 0.0 copy-start.3
  2.2 0.0 copy-start
  2.2 0.1 maximum_bitcast_fusion
  2.3 0.0 copy-start.1
  2.3 0.2 copy.22
  2.5 0.5 broadcast_select_fusion
  3.0 1.2 broadcast_select_fusion.2
  4.3 1.5 collective-permute-start
  5.7 0.0 copy-done.2
  5.7 0.0 copy-done.3
  5.7 0.1 select_reduce_fusion.1
  5.8 0.1 reshape.60
  6.0 0.1 fusion.1
  6.1 0.1 reshape.61
  6.3 0.2 slice_reduce_fusion
  6.5 0.6 dynamic_slice.3.len_ref
  7.1 0.0 copy-done
  7.1 0.6 reshape.67.ig_ref
  7.7 0.1 lt.31
  7.7 0.1 lt.32
  7.8 0.1 broadcast_in_dim.71
  7.9 0.1 broadcast_in_dim.72
  8.0 0.1 broadcast_in_dim.74
  8.2 0.7 reshape.71.tm_ref
  8.9 0.1 broadcast_in_dim.68
  8.9 0.1 broadcast_in_dim.69
  9.1 0.0 copy-done.1
  9.1 0.1 reshape.68
  9.2 0.7 reshape.69.tg_ref
  9.9 0.1 lt.29
  10.0 6.2 %copy.29 = bf16[128,384,38]{1,2,0:T(8,128)(2,1)} copy(bf16[128,384,38]{1,0,2:T(8,128)(2,1)} %param.10) | data formatting | bytes 7471104 | tf_op args[2]
  16.2 0.6 select_clamp_fusion
  16.8 0.0 collective-permute-done
  16.8 0.1 bitcast_add_fusion
  16.8 0.7 pad.23
  17.6 141.8 %joint_attention.1 = bf16[512,1280]{1,0:T(8,128)(2,1)} custom-call(s32[256]{0:T(256)} %get-tuple-element.12.src_ref, s32[256]{0:T(256)} %get-tuple-element.11.blk_ref, s32[4]{0:T(128)} %dynamic_slice.3.len_ref, bf16[9,3,40,128]{3,2,1,0:T(8,128)(2,1)} %bitcast.19, bf16[128,38,384]{2,1,0:T(8,128)(2,1)} %bitcast.16, bf16[512,2432]{1,0:T(8,128)(2,1)} %bitcast.18, ...), custom_call_target="tpu_custom_call" | custom-call | tf_op jit(solution)/shard_map/joint_attention/pallas_call | solution.py:424
  159.3 2.5 %copy.32 = bf16[2,256,1280]{2,1,0:T(8,128)(2,1)} copy(bf16[2,256,1280]{2,1,0:T(8,128)(2,1)} %bitcast.17) | data formatting | bytes 2621440
  (8 shorter events, 0.1 us)
Async XLA Ops:
  2.2 3.6 %copy-start.2 = (s32[1,128]{1,0:T(1,128)S(1)}, s32[1,128]{1,0:T(1,128)}, u32[]{:S(2)}) copy-start(s32[1,128]{1,0:T(1,128)} %param.12) | copy-start | bytes 1540
  2.2 3.6 %copy-start.3 = (s32[1,128]{1,0:T(1,128)S(1)}, s32[1,128]{1,0:T(1,128)}, u32[]{:S(2)}) copy-start(s32[1,128]{1,0:T(1,128)} %param.13) | copy-start | bytes 1540
  2.2 4.9 %copy-start = (f32[2432]{0:T(1024)S(1)}, f32[2432]{0:T(1024)}, u32[]{:S(2)}) copy-start(f32[2432]{0:T(1024)} %param.9) | copy-start | bytes 29188
  2.3 6.8 %copy-start.1 = (f32[2432]{0:T(1024)S(1)}, f32[2432]{0:T(1024)}, u32[]{:S(2)}) copy-start(f32[2432]{0:T(1024)} %param.11) | copy-start | bytes 29188
  4.3 12.5 %collective-permute-start = (bf16[25,40,128]{2,1,0:T(8,128)(2,1)S(1)}, bf16[25,40,128]{2,1,0:T(8,128)(2,1)S(1)}, u32[]{:S(2)}, u32[]{:S(2)}) collective-permute-start(bf16[25,40,128]{2,1,0:T(8,128)(2,1)S(1)} %bitcast.21), channel_id=1, source_target_pairs={{0,1},{1,0},{2,3},{3,2},{4,5},{5,4},{6,7},{7,6},{8,9},{9,8},{10,11... | collective-permute-start | bytes 768008 | tf_op jit(solution)/shard_map/ppermute | solution.py:466
